TPU v7x, 32 devices: a whole 2x2x4 slice. The times are simulated.
32 devices in a mesh: section: 2 (over core), dp: 8 (over z, x), rep: 2 (over y).
Axes of the slice: x: 2, y: 2, z: 4, core: 2. Of those that a mesh axis runs over, the one named last changes fastest.
Arguments:
- inputs: bfloat16 [4096, 1024], P(('dp', 'rep')), may hold values from -6 to 6
- cotangent: bfloat16 [4096, 1024], P(('dp', 'rep')), may hold values from -6 to 6
- seg_counts: int32 [256], P(('dp', 'rep')), may hold values from 2 to 16
- w_qkv: bfloat16 [2, 1024, 3072], P('section'), may hold values from -0.1875 to 0.1875
- w_out: bfloat16 [2, 1024, 1024], P('section'), may hold values from -0.375 to 0.375
- w_up: bfloat16 [2, 1024, 2048], P('section'), may hold values from -0.1875 to 0.1875
- w_down: bfloat16 [2, 2048, 1024], P('section'), may hold values from -0.1875 to 0.1875
- gains: float32 [2, 2, 1024], P('section'), may hold values from 0.5 to 1.5
- biases: float32 [2, 2, 1024], P('section'), may hold values from -3 to 3
Outputs:
- layer_outputs: bfloat16 [2, 4096, 1024], P('section', ('dp', 'rep'))
- input_grads: bfloat16 [2, 4096, 1024], P('section', ('dp', 'rep'))
- grad_qkv: float32 [2, 1024, 3072], P('section', 'dp')
- grad_wout: float32 [2, 1024, 1024], P('section', None, 'dp')
- grad_up: float32 [2, 1024, 2048], P('section', 'dp')
- grad_down: float32 [2, 2048, 1024], P('section', None, 'dp')
- grad_gains: float32 [2, 2, 1024], P('section', None, 'dp')
- grad_biases: float32 [2, 2, 1024], P('section', None, 'dp')
Inputs may be any that keep to these rules, and one draw needn't show every extreme that they name: seg_counts gives each series' number of valid slots; the first 16 - seg_counts slots of a series are padding.
All inputs are finite; a program needn't handle non-finite values.
Results may differ from a plain program's by a relative error of at most 0.015.
Values may be sent and summed in bfloat16 or wider, within the bound.
A program may use at most 256 MiB of HBM per device.

v0:
```python
from functools import partial

import jax
import jax.numpy as jnp
from jax import lax
from jax.experimental import pallas as pl
from jax.experimental.pallas import tpu as pltpu
from jax.sharding import PartitionSpec as P

SEG = 16
HEAD = 128
BLOCK = 128
TILE = 512
MESH = pl.DeviceIdType.MESH
epsilon = 1e-05
f32 = jnp.float32
bf16 = jnp.bfloat16
NN = (((1,), (0,)), ((), ()))
NT = (((1,), (1,)), ((), ()))
TN = (((0,), (0,)), ((), ()))


def mul(left, right, dims=NN):
    return lax.dot_general(left, right, dims, preferred_element_type=f32)


def normalize(hidden):
    average = jnp.mean(hidden, axis=-1, keepdims=True)
    centred = hidden - average
    inverse = lax.rsqrt(jnp.mean(centred * centred, axis=-1, keepdims=True) + epsilon)
    return (centred * inverse, inverse)


def normalize_back(grad_normed, normed, inverse):
    centre_term = jnp.mean(grad_normed, axis=-1, keepdims=True)
    slope_term = normed * jnp.mean(grad_normed * normed, axis=-1, keepdims=True)
    return inverse * (grad_normed - centre_term - slope_term)


def gelu_pair(u):
    k = 0.7978845608
    square = u * u
    t = jnp.tanh(k * (u + 0.044715 * u * square))
    half = 0.5 * (1.0 + t)
    slope = half + 0.5 * u * (1.0 - t * t) * (k * (1.0 + 3 * 0.044715 * square))
    return u * half, slope


def step_kernel(
    n1, n2, x_ref, ct_ref, count_ref, wq_hbm, wo_hbm, wu_hbm, wd_hbm, gain_ref, bias_ref,
    out_ref, dh_ref, gq_ref, go_ref, gu_ref, gd_ref, small_ref,
    wq, wo, wu, wd, hb, eb, norm1, norm2, inv1, inv2, ab, pb, cb, dmb, dob, probs, mm, gp, dcb, acc, mask,
    lt, ltr, ra, rr, xs, xr, zs, zr, own, ag, sx, sz, sy,
    w_sem, y_send, y_recv, x_send, x_recv, z_send, z_recv, g_send, g_recv, s_send, s_recv, p_send, p_recv,
):
    dp = n1 * n2
    rows, width = hb.shape
    blocks = rows // BLOCK
    heads = width // HEAD
    ff = wu.shape[1]
    shard = width // dp
    tiles = ra.shape[0] // 2
    scale = HEAD**-0.5
    sec = lax.axis_index("section")
    me = lax.axis_index("dp")
    rep = lax.axis_index("rep")
    hi, lo = me // n1, me % n1
    other = 1 - rep
    y_to = (sec, me, other)
    s_to = (1 - sec, me, rep)

    def x_to(k):
        return (sec, hi * n1 + (lo + k) % n1, rep)

    def z_to(k):
        return (sec, ((hi + k) % n2) * n1 + lo, rep)

    weights = [
        pltpu.make_async_copy(src.at[0], dst, w_sem.at[i])
        for i, (src, dst) in enumerate(((wq_hbm, wq), (wo_hbm, wo), (wu_hbm, wu), (wd_hbm, wd)))
    ]
    for copy in weights:
        copy.start()

    barrier = pltpu.get_barrier_semaphore()
    peers = [s_to, y_to] + [x_to(k) for k in range(1, n1)] + [z_to(k) for k in range(1, n2)]
    for peer in peers:
        pl.semaphore_signal(barrier, inc=1, device_id=peer, device_id_type=MESH)
    pl.semaphore_wait(barrier, len(peers))

    q_tiles, o_tiles, u_tiles = 3 * width // TILE, width // TILE, ff // TILE
    O_AT, U_AT, G_AT = q_tiles, tiles, tiles + u_tiles

    def early(r):
        return jnp.where(r == 0, o_tiles, u_tiles)

    def rhs_of(r, t):
        return r * tiles + (t + tiles - early(r)) % tiles

    def lhs_of(r, t):
        return jnp.where(t < early(r), 1, 0)

    def remote(src, dst, ss, rs, to):
        return pltpu.make_async_remote_copy(
            src_ref=src, dst_ref=dst, send_sem=ss, recv_sem=rs, device_id=to, device_id_type=MESH
        )

    def forward_hop():
        return remote(out_ref, hb, p_send.at[0], p_recv.at[0], s_to)

    def backward_hop():
        return remote(dh_ref, eb, p_send.at[1], p_recv.at[1], s_to)

    def y_lhs(h):
        return remote(lt.at[2 * other + h], ltr.at[h], y_send.at[tiles + h], y_recv.at[tiles + h], y_to)

    def y_tile(t):
        return remote(ra.at[rhs_of(other, t)], rr.at[t], y_send.at[t], y_recv.at[t], y_to)

    def x_tile(k, t):
        return remote(xs.at[k - 1, t], xr.at[k - 1, t], x_send.at[k - 1, t], x_recv.at[k - 1, t], x_to(k))

    def z_tile(k, t):
        return remote(
            zs.at[t, (hi + k) % n2], zr.at[k - 1, t], z_send.at[k - 1, t], z_recv.at[k - 1, t], z_to(k)
        )

    def g_tile(t):
        return remote(ag.at[rep, t], ag.at[rep, t], g_send.at[t], g_recv.at[t], y_to)

    def small_x(k):
        return remote(sx.at[0], sx.at[k], s_send.at[k - 1], s_recv.at[k - 1], x_to(k))

    def small_z(k):
        n = n1 - 1 + k - 1
        return remote(sz.at[0], sz.at[k], s_send.at[n], s_recv.at[n], z_to(k))

    def small_y():
        n = n1 + n2 - 2
        return remote(sy.at[0], sy.at[1], s_send.at[n], s_recv.at[n], y_to)

    def transpose_into(m, ref):
        for b in range(width // 128):
            block = ref[:, b * 128 : (b + 1) * 128].T
            size = min(shard, 128)
            for q in range(128 // size):
                first = b * 128 + q * size
                j = first // shard
                at = (j // n1) * shard + first % shard
                lt[m, j % n1, at : at + size, :] = block[q * size : (q + 1) * size]

    row_at = lax.broadcasted_iota(jnp.int32, (BLOCK, BLOCK), 0)
    col_at = lax.broadcasted_iota(jnp.int32, (BLOCK, BLOCK), 1)
    base = (row_at // SEG == col_at // SEG) & (col_at <= row_at)
    per = BLOCK // SEG
    for b in range(blocks):
        first = jnp.zeros((BLOCK, BLOCK), jnp.int32)
        for j in range(per):
            first = jnp.where(col_at // SEG == j, SEG - count_ref[b * per + j], first)
        allowed = base & ((col_at % SEG >= first) | (col_at == row_at))
        mask[b] = jnp.where(allowed, 1.0, 0.0)
    acc[...] = jnp.zeros_like(acc)

    LN = 32

    def row_loop(body):
        def run(i, carry):
            body(pl.ds(pl.multiple_of(i * LN, LN), LN))
            return carry

        lax.fori_loop(0, rows // LN, run, 0)

    def tile_loop(count, body):
        def run(t, carry):
            body(t, pl.ds(pl.multiple_of(t * TILE, TILE), TILE))
            return carry

        lax.fori_loop(0, count, run, 0)

    @pl.when(sec == 0)
    def _():
        hb[...] = x_ref[...]

    @pl.when(sec == 1)
    def _():
        eb[...] = ct_ref[...]
        transpose_into(3, eb)

        @pl.when(rep == 0)
        def _():
            y_lhs(1).start()

        forward_hop().wait_recv()

    def first_norm(at):
        normed, inverse = normalize(hb[at].astype(f32))
        norm1[at] = normed
        inv1[at] = inverse
        ab[at] = (normed * gain_ref[0, 0:1] + bias_ref[0, 0:1]).astype(bf16)

    row_loop(first_norm)
    weights[0].wait()

    def project(t, at):
        pb[:, at] = mul(ab[...], wq[:, at]).astype(bf16)

    tile_loop(q_tiles, project)

    def head_loop(body):
        def run(i, carry):
            for b in range(blocks):
                for u in range(2):
                    body(b, 2 * i + u)
            return carry

        lax.fori_loop(0, heads // 2, run, 0)

    def part(b, member, h):
        return pb[b * BLOCK : (b + 1) * BLOCK, pl.ds(pl.multiple_of(member * width + h * HEAD, HEAD), HEAD)]

    def tile_at(first, b, h):
        per_tile = TILE // HEAD
        cols = pl.ds(pl.multiple_of((h % per_tile) * HEAD, HEAD), HEAD)
        return (first + h // per_tile, pl.ds(b * BLOCK, BLOCK), cols)

    def attend(b, h):
        scores = mul(part(b, 0, h), part(b, 1, h), NT) * scale
        scores = jnp.where(mask[b] > 0.5, scores, -1e30)
        raised = jnp.exp(scores - jnp.max(scores, axis=-1, keepdims=True))
        chance = raised * (1.0 / jnp.sum(raised, axis=-1, keepdims=True))
        probs[b, h] = chance
        ra[tile_at(O_AT, b, h)] = mul(chance.astype(bf16), part(b, 2, h)).astype(bf16)

    head_loop(attend)
    weights[1].wait()

    def attention_out(t, at):
        total = hb[:, at].astype(f32)
        for k in range(o_tiles):
            total = total + mul(ra[O_AT + k], wo[k * TILE : (k + 1) * TILE, at])
        mm[:, at] = total

    tile_loop(o_tiles, attention_out)

    def second_norm(at):
        normed, inverse = normalize(mm[at])
        norm2[at] = normed
        inv2[at] = inverse
        cb[at] = (normed * gain_ref[0, 1:2] + bias_ref[0, 1:2]).astype(bf16)

    row_loop(second_norm)
    weights[2].wait()

    def feed_up(t, at):
        upper = mul(cb[...], wu[:, at])
        value, slope = gelu_pair(upper)
        ra[G_AT + t] = value.astype(bf16)
        gp[:, at] = slope

    tile_loop(u_tiles, feed_up)
    weights[3].wait()

    def feed_down(t, at):
        total = mm[:, at]
        for k in range(u_tiles):
            total = total + mul(ra[G_AT + k], wd[k * TILE : (k + 1) * TILE, at])
        out_ref[:, at] = total.astype(bf16)

    tile_loop(o_tiles, feed_down)

    @pl.when(sec == 0)
    def _():
        forward_hop().start()

    transpose_into(2, cb)

    @pl.when(rep == 0)
    def _():
        for t in range(u_tiles):
            y_tile(t).start()
        y_lhs(0).start()

    transpose_into(0, ab)

    @pl.when(rep == 1)
    def _():
        for t in range(o_tiles):
            y_tile(t).start()
        y_lhs(0).start()

    @pl.when(sec == 0)
    def _():
        backward_hop().wait_recv()
        transpose_into(3, eb)

        @pl.when(rep == 0)
        def _():
            y_lhs(1).start()

    def feed_down_back(t, at):
        ra[U_AT + t] = (mul(eb[...], wd[at, :], NT) * gp[:, at]).astype(bf16)

    tile_loop(u_tiles, feed_down_back)

    @pl.when(rep == 0)
    def _():
        for t in range(u_tiles, tiles):
            y_tile(t).start()

    def feed_up_back(t, at):
        total = mul(ra[U_AT], wu[at, 0:TILE], NT)
        for k in range(1, u_tiles):
            total = total + mul(ra[U_AT + k], wu[at, k * TILE : (k + 1) * TILE], NT)
        dcb[:, at] = total

    tile_loop(o_tiles, feed_up_back)

    def add_rows(i, value):
        acc[i] += jnp.sum(value.reshape(LN // 8, 8, width), axis=0)

    def second_back(at):
        d_c, normed = dcb[at], norm2[at]
        add_rows(1, d_c * normed)
        add_rows(3, d_c)
        d_m = eb[at].astype(f32) + normalize_back(d_c * gain_ref[0, 1:2], normed, inv2[at])
        mm[at] = d_m
        dmb[at] = d_m.astype(bf16)

    row_loop(second_back)

    def attention_out_back(t, at):
        dob[:, at] = mul(dmb[...], wo[at, :], NT).astype(bf16)

    tile_loop(o_tiles, attention_out_back)
    transpose_into(1, dmb)

    @pl.when(rep == 1)
    def _():
        y_lhs(1).start()

    def attend_back(b, h):
        d_o = dob[b * BLOCK : (b + 1) * BLOCK, pl.ds(pl.multiple_of(h * HEAD, HEAD), HEAD)]
        q, k, v = part(b, 0, h), part(b, 1, h), part(b, 2, h)
        chance = probs[b, h]
        d_probs = mul(d_o, v, NT)
        d_s = (chance * (d_probs - jnp.sum(chance * d_probs, axis=-1, keepdims=True))).astype(bf16)
        ra[tile_at(0, b, h)] = (mul(d_s, k) * scale).astype(bf16)
        ra[tile_at(o_tiles, b, h)] = (mul(d_s, q, TN) * scale).astype(bf16)
        ra[tile_at(2 * o_tiles, b, h)] = mul(chance.astype(bf16), d_o, TN).astype(bf16)

    head_loop(attend_back)

    @pl.when(rep == 1)
    def _():
        for t in range(o_tiles, tiles):
            y_tile(t).start()

    def project_back(t, at):
        total = mul(ra[0], wq[at, 0:TILE], NT)
        for k in range(1, q_tiles):
            total = total + mul(ra[k], wq[at, k * TILE : (k + 1) * TILE], NT)
        dcb[:, at] = total

    tile_loop(o_tiles, project_back)

    def first_back(at):
        d_a, normed = dcb[at], norm1[at]
        add_rows(0, d_a * normed)
        add_rows(2, d_a)
        d_h = mm[at] + normalize_back(d_a * gain_ref[0, 0:1], normed, inv1[at])
        dh_ref[at] = d_h.astype(bf16)

    row_loop(first_back)

    @pl.when(sec == 1)
    def _():
        backward_hop().start()

    def product(t, which):
        h, r = lhs_of(rep, t), rhs_of(rep, t)
        return mul(lt[2 * rep + h, which], ra[r]) + mul(ltr[h, which], rr[t])

    def stage_a(t):
        for h in range(2):

            @pl.when(t == (0 if h == 1 else early(rep)))
            def _():
                y_lhs(h).wait_recv()

        y_tile(t).wait_recv()
        for k in range(1, n1):
            part_sum = product(t, (lo + k) % n1).astype(bf16)
            for q in range(n2):
                xs[k - 1, t, q] = part_sum[q * shard : (q + 1) * shard]
            x_tile(k, t).start()

    def stage_b(t):
        part_sum = product(t, lo)
        for k in range(1, n1):
            x_tile(k, t).wait_recv()
        for q in range(n2):
            total = part_sum[q * shard : (q + 1) * shard]
            for k in range(1, n1):
                total = total + xr[k - 1, t, q].astype(f32)
            zs[t, q] = total.astype(bf16)

            @pl.when(hi == q)
            def _():
                own[t] = total

        for k in range(1, n2):
            z_tile(k, t).start()

    def stage_c(t):
        total = own[t]
        for k in range(1, n2):
            z_tile(k, t).wait_recv()
            total = total + zr[k - 1, t].astype(f32)
        ag[rep, t] = total.astype(bf16)
        g_tile(t).start()

    def reduce_step(s, carry):
        for lag, stage in ((0, stage_a), (2, stage_b), (4, stage_c)):

            @pl.when((s >= lag) & (s < tiles + lag))
            def _():
                stage(s - lag)

        return carry

    lax.fori_loop(0, tiles + 4, reduce_step, 0)

    for i in range(4):
        sx[0, i : i + 1] = jnp.sum(acc[i], axis=0, keepdims=True)
        sx[0, 4 + i : 5 + i] = jnp.zeros((1, width), f32)
    for k in range(1, n1):
        small_x(k).start()
    total = sx[0]
    for k in range(1, n1):
        small_x(k).wait_recv()
        total = total + sx[k]
    sz[0] = total
    for k in range(1, n2):
        small_z(k).start()
    for k in range(1, n2):
        small_z(k).wait_recv()
        total = total + sz[k]
    sy[0] = total
    small_y().start()
    small_y().wait_recv()
    sy[2] = sy[0] + sy[1]
    if shard % 128 == 0:
        small_ref[...] = sy[2, :, pl.ds(pl.multiple_of(me * shard, shard), shard)]
    else:
        small_ref[...] = sy[2]

    for t in range(tiles):
        g_tile(t).wait_recv()
        c = (t + tiles - o_tiles) % tiles
        if c < q_tiles:
            gq_ref[:, c * TILE : (c + 1) * TILE] = ag[0, t]
        elif shard % 128 == 0:
            go_ref[(c - q_tiles) * TILE : (c - q_tiles + 1) * TILE, :] = ag[0, t].T
        else:
            go_ref[:, (c - q_tiles) * TILE : (c - q_tiles + 1) * TILE] = ag[0, t]
        c = (t + tiles - u_tiles) % tiles
        if c < u_tiles:
            gu_ref[:, c * TILE : (c + 1) * TILE] = ag[1, t]
        elif shard % 128 == 0:
            gd_ref[(c - u_tiles) * TILE : (c - u_tiles + 1) * TILE, :] = ag[1, t].T
        else:
            gd_ref[:, (c - u_tiles) * TILE : (c - u_tiles + 1) * TILE] = ag[1, t]

    def drain(t, carry):
        y_tile(t).wait_send()
        for k in range(1, n1):
            x_tile(k, t).wait_send()
        for k in range(1, n2):
            z_tile(k, t).wait_send()
        g_tile(t).wait_send()
        return carry

    lax.fori_loop(0, tiles, drain, 0)
    for h in range(2):
        y_lhs(h).wait_send()
    for k in range(1, n1):
        small_x(k).wait_send()
    for k in range(1, n2):
        small_z(k).wait_send()
    small_y().wait_send()

    @pl.when(sec == 0)
    def _():
        forward_hop().wait_send()

    @pl.when(sec == 1)
    def _():
        backward_hop().wait_send()


def per_device(inputs, cotangent, seg_counts, w_qkv, w_out, w_up, w_down, gains, biases):
    dp = lax.axis_size("dp")
    n1 = 2 if dp < 16 else 4
    n2 = dp // n1
    rows, width = inputs.shape
    ff = w_up.shape[2]
    shard = width // dp
    direct = shard % 128 == 0
    tiles = 2 * ff // TILE
    blocks, heads = rows // BLOCK, width // HEAD
    o_tiles = width // TILE
    dma = pltpu.SemaphoreType.DMA
    vm = pltpu.VMEM
    act = vm((rows, width), bf16)
    wide = vm((rows, width), f32)
    scratch = [
        vm((width, 3 * width), bf16), vm((width, width), bf16), vm((width, ff), bf16), vm((ff, width), bf16),
        act, act, wide, wide, vm((rows, 1), f32), vm((rows, 1), f32),
        act, vm((rows, 3 * width), bf16), act, act, act,
        vm((blocks, heads, BLOCK, BLOCK), f32), wide, vm((rows, ff), f32), wide,
        vm((4, 8, width), f32), vm((blocks, BLOCK, BLOCK), f32),
        vm((4, n1, n2 * shard, rows), bf16),
        vm((2, n1, n2 * shard, rows), bf16),
        vm((2 * tiles, rows, TILE), bf16),
        vm((tiles, rows, TILE), bf16),
        vm((n1 - 1, tiles, n2, shard, TILE), bf16),
        vm((n1 - 1, tiles, n2, shard, TILE), bf16),
        vm((tiles, n2, shard, TILE), bf16),
        vm((n2 - 1, tiles, shard, TILE), bf16),
        vm((tiles, shard, TILE), f32),
        vm((2, tiles, shard, TILE), bf16),
        vm((n1, 8, width), f32), vm((n2, 8, width), f32), vm((3, 8, width), f32),
        dma((4,)),
        dma((tiles + 2,)), dma((tiles + 2,)),
        dma((n1 - 1, tiles)), dma((n1 - 1, tiles)),
        dma((n2 - 1, tiles)), dma((n2 - 1, tiles)),
        dma((tiles,)), dma((tiles,)),
        dma((n1 + n2 - 1,)), dma((n1 + n2 - 1,)),
        dma((2,)), dma((2,)),
    ]
    vspec = pl.BlockSpec(memory_space=pltpu.VMEM)
    hbm = pl.BlockSpec(memory_space=pl.ANY)
    sds = jax.ShapeDtypeStruct
    turned = (lambda n: (n, shard)) if direct else (lambda n: (shard, n))
    out, d_h, g_q, g_o, g_u, g_d, small = pl.pallas_call(
        partial(step_kernel, n1, n2),
        out_shape=(
            sds((rows, width), bf16), sds((rows, width), bf16),
            sds((shard, 3 * width), bf16), sds(turned(width), bf16),
            sds((shard, ff), bf16), sds(turned(ff), bf16),
            sds((8, shard if direct else width), f32),
        ),
        in_specs=[vspec, vspec, pl.BlockSpec(memory_space=pltpu.SMEM)] + [hbm] * 4 + [vspec] * 2,
        out_specs=(vspec,) * 7,
        scratch_shapes=scratch,
        name="layers_step",
        compiler_params=pltpu.CompilerParams(
            collective_id=0, has_side_effects=True, vmem_limit_bytes=67043328
        ),
    )(inputs, cotangent, seg_counts, w_qkv, w_out, w_up, w_down, gains, biases)
    if not direct:
        g_o, g_d = g_o.T, g_d.T
        small = lax.dynamic_slice_in_dim(small, lax.axis_index("dp") * shard, shard, 1)
    grads = [g.astype(f32)[None] for g in (g_q, g_o, g_u, g_d)]
    return (out[None], d_h[None], *grads, small[None, 0:2], small[None, 2:4])


def solution(mesh):
    rows = P(("dp", "rep"), None)
    layer = P("section", None, None)
    return jax.shard_map(
        per_device,
        mesh=mesh,
        in_specs=(rows, rows, P(("dp", "rep"))) + (layer,) * 6,
        out_specs=(
            P("section", ("dp", "rep"), None),
            P("section", ("dp", "rep"), None),
            P("section", "dp", None),
            P("section", None, "dp"),
            P("section", "dp", None),
            P("section", None, "dp"),
            P("section", None, "dp"),
            P("section", None, "dp"),
        ),
        check_vma=False,
    )
```

profile of v0, /device:TPU:0, one launch (start us, length us, event | category | flops | bytes accessed | tf_op | source)
XLA Modules:
  0.0 188.7 jit_solution(11227478953324363003)
XLA Ops:
  0.6 178.7 %layers_step.1 = (bf16[256,1024]{1,0:T(8,128)(2,1)}, bf16[256,1024]{1,0:T(8,128)(2,1)}, bf16[128,3072]{1,0:T(8,128)(2,1)}, bf16[1024,128]{1,0:T(8,128)(2,1)}, bf...) custom-call(bf16[256,1024]{1,0:T(8,128)(2,1)} %x_ref.1, bf16[256,1024]{1,0:T(8,128)(2,1)} %ct_ref.1, ...), custom_call_target="tpu_custom_call" | custom-call | tf_op jit(solution)/shard_map/layers_step/pallas_call | solution.py:545
  179.3 0.0 copy-start
  179.3 0.0 copy-start.3
  179.3 0.0 copy-start.2
  179.3 0.0 copy-start.1
  179.3 1.4 slice_bitcast_fusion
  180.7 2.4 %bitcast_convert_fusion = f32[1,128,3072]{2,1,0:T(8,128)} fusion(bf16[128,3072]{1,0:T(8,128)(2,1)} %get-tuple-element.17), kind=kLoop, calls=%fused_computation | loop fusion | flops 393216 | bytes 2359296 | tf_op jit(solution)/shard_map/broadcast_in_dim | solution.py:564
  183.2 2.1 %bitcast_convert_fusion.1 = f32[1,2048,128]{2,1,0:T(8,128)} fusion(bf16[2048,128]{1,0:T(8,128)(2,1)} %get-tuple-element.20), kind=kLoop, calls=%fused_computation.1 | loop fusion | flops 262144 | bytes 1572864 | tf_op jit(solution)/shard_map/broadcast_in_dim | solution.py:564
  185.2 0.0 copy-done
  185.2 1.1 bitcast_convert_fusion.2
  186.3 0.0 copy-done.3
  186.3 0.8 bitcast_convert_fusion.3
  187.1 0.0 copy-done.2
  187.1 0.8 copy.19
  187.9 0.0 copy-done.1
  187.9 0.8 copy.20
Async XLA Ops:
  179.3 5.9 %copy-start = (bf16[128,2048]{1,0:T(8,128)(2,1)S(1)}, bf16[128,2048]{1,0:T(8,128)(2,1)}, u32[]{:S(2)}) copy-start(bf16[128,2048]{1,0:T(8,128)(2,1)} %get-tuple-element.19) | copy-start | bytes 1572868
  179.3 7.0 %copy-start.3 = (bf16[1024,128]{1,0:T(8,128)(2,1)S(1)}, bf16[1024,128]{1,0:T(8,128)(2,1)}, u32[]{:S(2)}) copy-start(bf16[1024,128]{1,0:T(8,128)(2,1)} %get-tuple-element.18) | copy-start | bytes 786436
  179.3 7.8 %copy-start.2 = (bf16[256,1024]{1,0:T(8,128)(2,1)S(1)}, bf16[256,1024]{1,0:T(8,128)(2,1)}, u32[]{:S(2)}) copy-start(bf16[256,1024]{1,0:T(8,128)(2,1)} %get-tuple-element.15) | copy-start | bytes 1572868
  179.3 8.6 %copy-start.1 = (bf16[256,1024]{1,0:T(8,128)(2,1)S(1)}, bf16[256,1024]{1,0:T(8,128)(2,1)}, u32[]{:S(2)}) copy-start(bf16[256,1024]{1,0:T(8,128)(2,1)} %get-tuple-element.16) | copy-start | bytes 1572868
where the time goes:
time: 189 us
  Pallas kernels  179 us (95%)
  other arithmetic  6.41 us (3%)
  local copies, waits for them, and re-layouts  2.98 us (2%)
    pallas_call x1, Pallas kernels, per_device(): pl.pallas_call(partial(step_kernel, n1, n2), out_shape=(sds((rows, width)...  179 us
    broadcast_in_dim x4, other arithmetic, per_device(): grads = [g.astype(f32)[None] for g in (g_q, g_o, g_u, g_d)]  6.41 us

commit v1 on v0

v1 whole, which is shorter than its diff:
```python
from functools import partial

import jax
import jax.numpy as jnp
from jax import lax
from jax.experimental import pallas as pl
from jax.experimental.pallas import tpu as pltpu
from jax.sharding import PartitionSpec as P

SEG = 16
HEAD = 128
BLOCK = 128
TILE = 512
CUT = 256
MESH = pl.DeviceIdType.MESH
epsilon = 1e-05
f32 = jnp.float32
bf16 = jnp.bfloat16
NN = (((1,), (0,)), ((), ()))
NT = (((1,), (1,)), ((), ()))
TN = (((0,), (0,)), ((), ()))


def mul(left, right, dims=NN):
    return lax.dot_general(left, right, dims, preferred_element_type=f32)


def normalize(hidden):
    average = jnp.mean(hidden, axis=-1, keepdims=True)
    centred = hidden - average
    inverse = lax.rsqrt(jnp.mean(centred * centred, axis=-1, keepdims=True) + epsilon)
    return (centred * inverse, inverse)


def normalize_back(grad_normed, normed, inverse):
    centre_term = jnp.mean(grad_normed, axis=-1, keepdims=True)
    slope_term = normed * jnp.mean(grad_normed * normed, axis=-1, keepdims=True)
    return inverse * (grad_normed - centre_term - slope_term)


def gelu_pair(u):
    k = 0.7978845608
    square = u * u
    t = jnp.tanh(k * (u + 0.044715 * u * square))
    half = 0.5 * (1.0 + t)
    slope = half + 0.5 * u * (1.0 - t * t) * (k * (1.0 + 3 * 0.044715 * square))
    return u * half, slope


def step_kernel(
    x_hbm, ct_hbm, count_ref, wq_hbm, wo_hbm, wu_hbm, wd_hbm, gain_ref, bias_ref,
    out_hbm, dh_hbm, grad_hbm, small_ref,
    wq, wo, wu, wd, hb, eb, norm1, norm2, inv1, inv2, ab, pb, cb, dmb, dob, probs, mm, gp, dcb, acc, mask,
    mask2, pin, out_ref, dh_ref, lt, ltr, ra, rr, ag, small, *rest,
):
    dp = lt.shape[1] * lt.shape[2]
    levels = dp.bit_length() - 1
    sends, arrivals = rest[:levels], rest[levels : 2 * levels]
    w_sem, o_sem, y_send, y_recv, x_send, x_recv, g_send, g_recv, s_send, s_recv, p_send, p_recv = rest[2 * levels :]
    rows, width = hb.shape
    blocks = rows // BLOCK
    heads = width // HEAD
    ff = wu.shape[1]
    shard = width // dp
    tiles = ra.shape[0] // 2
    cuts = ag.shape[1]
    per_tile = cuts // tiles
    scale = HEAD**-0.5
    sec = lax.axis_index("section")
    me = lax.axis_index("dp")
    rep = lax.axis_index("rep")
    other = 1 - rep
    y_to = (sec, me, other)
    s_to = (1 - sec, me, rep)

    def x_to(bit):
        stride = 1 << bit
        return (sec, me + stride - 2 * stride * (me // stride % 2), rep)

    weights = [
        pltpu.make_async_copy(src.at[0], dst, w_sem.at[i])
        for i, (src, dst) in enumerate(((wq_hbm, wq), (wo_hbm, wo), (wu_hbm, wu), (wd_hbm, wd)))
    ]
    take_x = pltpu.make_async_copy(x_hbm, hb, o_sem.at[3])
    take_ct = pltpu.make_async_copy(ct_hbm, eb, o_sem.at[3])

    @pl.when(sec == 0)
    def _():
        take_x.start()

    @pl.when(sec == 1)
    def _():
        take_ct.start()

    for copy in weights:
        copy.start()

    barrier = pltpu.get_barrier_semaphore()
    peers = [s_to, y_to] + [x_to(bit) for bit in range(levels)]
    for peer in peers:
        pl.semaphore_signal(barrier, inc=1, device_id=peer, device_id_type=MESH)
    pl.semaphore_wait(barrier, len(peers))

    q_tiles, o_tiles, u_tiles = 3 * width // TILE, width // TILE, ff // TILE
    O_AT, U_AT, G_AT = q_tiles, tiles, tiles + u_tiles

    def early(r):
        return jnp.where(r == 0, o_tiles, u_tiles)

    def rhs_of(r, t):
        return r * tiles + (t + tiles - early(r)) % tiles

    def lhs_of(r, t):
        return jnp.where(t < early(r), 1, 0)

    def remote(src, dst, ss, rs, to):
        return pltpu.make_async_remote_copy(
            src_ref=src, dst_ref=dst, send_sem=ss, recv_sem=rs, device_id=to, device_id_type=MESH
        )

    def forward_hop():
        return remote(out_ref, hb, p_send.at[0], p_recv.at[0], s_to)

    def backward_hop():
        return remote(dh_ref, eb, p_send.at[1], p_recv.at[1], s_to)

    def y_hop(n, src, dst):
        return remote(src, dst, y_send.at[n], y_recv.at[n], y_to)

    def y_act(h, src):
        return y_hop(h, src, pin.at[h])

    def y_mask():
        return y_hop(2, mask, mask2)

    def y_mixed(t):
        return y_hop(3 + t, ra.at[O_AT + t], rr.at[t])

    def bit_of(level, t):
        return jnp.where(t % 3 == 2, 1 - level, level) if level < 2 else level

    def half_of(level, t):
        return me // (1 << bit_of(level, t)) % 2 if level >= 2 else jnp.where(bit_of(level, t) == 0, me % 2, me // 2 % 2)

    def peer_of(level, t):
        stride = jnp.where(bit_of(level, t) == 0, 1, 2) if level < 2 else 1 << level
        return (sec, me + stride - 2 * stride * half_of(level, t), rep)

    def x_tile(level, t):
        return remote(
            sends[level].at[t, 1 - half_of(level, t)] if level else sends[0].at[t],
            arrivals[level].at[t], x_send.at[level, t], x_recv.at[level, t], peer_of(level, t),
        )

    def g_tile(t):
        return remote(ag.at[rep, t], ag.at[rep, t], g_send.at[t], g_recv.at[t], y_to)

    def small_hop(n):
        to = x_to(n) if n < levels else y_to
        return remote(small.at[2 * n], small.at[2 * n + 1], s_send.at[n], s_recv.at[n], to)

    def transpose_into(lt, m, ref):
        for b in range(width // 128):
            block = ref[:, b * 128 : (b + 1) * 128].T
            size = min(shard, 128)
            for q in range(128 // size):
                first = b * 128 + q * size
                j = first // shard
                lt[m, j % 2, j // 2, first % shard : first % shard + size, :] = block[q * size : (q + 1) * size]

    row_at = lax.broadcasted_iota(jnp.int32, (BLOCK, BLOCK), 0)
    col_at = lax.broadcasted_iota(jnp.int32, (BLOCK, BLOCK), 1)
    base = (row_at // SEG == col_at // SEG) & (col_at <= row_at)
    per = BLOCK // SEG
    for b in range(blocks):
        first = jnp.zeros((BLOCK, BLOCK), jnp.int32)
        for j in range(per):
            first = jnp.where(col_at // SEG == j, SEG - count_ref[b * per + j], first)
        allowed = base & ((col_at % SEG >= first) | (col_at == row_at))
        mask[b] = jnp.where(allowed, 1.0, 0.0)
    acc[...] = jnp.zeros_like(acc)

    LN = 128

    def row_loop(body):
        def run(i, carry):
            body(pl.ds(pl.multiple_of(i * LN, LN), LN))
            return carry

        lax.fori_loop(0, rows // LN, run, 0)

    def tile_loop(count, body):
        def run(t, carry):
            body(t, pl.ds(pl.multiple_of(t * TILE, TILE), TILE))
            return carry

        lax.fori_loop(0, count, run, 0)

    y_mask().start()

    def share_grad():
        @pl.when(rep == 0)
        def _():
            y_act(1, eb).start()

        @pl.when(rep == 1)
        def _():
            transpose_into(lt, 1, eb)

    @pl.when(sec == 0)
    def _():
        take_x.wait()

    @pl.when(sec == 1)
    def _():
        take_ct.wait()
        share_grad()
        forward_hop().wait_recv()

    def first_norm(at):
        normed, inverse = normalize(hb[at].astype(f32))
        norm1[at] = normed
        inv1[at] = inverse
        ab[at] = (normed * gain_ref[0, 0:1] + bias_ref[0, 0:1]).astype(bf16)

    row_loop(first_norm)

    @pl.when(rep == 1)
    def _():
        y_act(0, ab).start()

    weights[0].wait()

    def project(source):
        def run(t, at):
            pb[:, at] = mul(source(), wq[:, at]).astype(bf16)

        tile_loop(q_tiles, run)

    project(lambda: ab[...])

    def head_loop(body):
        def run(i, carry):
            body([(b, i * 8 + u) for u in range(8) for b in range(blocks)])
            return carry

        lax.fori_loop(0, heads // 8, run, 0)

    def part(b, member, h):
        return pb[b * BLOCK : (b + 1) * BLOCK, pl.ds(pl.multiple_of(member * width + h * HEAD, HEAD), HEAD)]

    def tile_at(first, b, h):
        group = TILE // HEAD
        cols = pl.ds(pl.multiple_of((h % group) * HEAD, HEAD), HEAD)
        return (first + h // group, pl.ds(b * BLOCK, BLOCK), cols)

    def chances_of(pairs, mask):
        scores = [mul(part(b, 0, h), part(b, 1, h), NT) for b, h in pairs]
        chances = []
        for (b, h), score in zip(pairs, scores):
            score = jnp.where(mask[b] > 0.5, score * scale, -1e30)
            raised = jnp.exp(score - jnp.max(score, axis=-1, keepdims=True))
            chance = raised * (1.0 / jnp.sum(raised, axis=-1, keepdims=True))
            probs[b, h] = chance
            chances.append(chance.astype(bf16))
        return chances

    def attend(pairs):
        for (b, h), chance in zip(pairs, chances_of(pairs, mask)):
            ra[tile_at(O_AT, b, h)] = mul(chance, part(b, 2, h)).astype(bf16)

    head_loop(attend)

    @pl.when(rep == 1)
    def _():
        for t in range(o_tiles):
            y_mixed(t).start()

    weights[1].wait()

    def attention_out(t, at):
        total = hb[:, at].astype(f32)
        for k in range(o_tiles):
            total = total + mul(ra[O_AT + k], wo[k * TILE : (k + 1) * TILE, at])
        mm[:, at] = total

    tile_loop(o_tiles, attention_out)

    def second_norm(at):
        normed, inverse = normalize(mm[at])
        norm2[at] = normed
        inv2[at] = inverse
        cb[at] = (normed * gain_ref[0, 1:2] + bias_ref[0, 1:2]).astype(bf16)

    row_loop(second_norm)

    @pl.when(rep == 0)
    def _():
        y_act(0, cb).start()

    weights[2].wait()

    def feed_up(t, at, source, store, first):
        value, slope = gelu_pair(mul(source[...], wu[:, at]))
        store[first + t] = value.astype(bf16)
        gp[:, at] = slope

    tile_loop(u_tiles, partial(feed_up, source=cb, store=ra, first=G_AT))
    weights[3].wait()

    def feed_down(t, at):
        total = mm[:, at]
        for k in range(u_tiles):
            total = total + mul(ra[G_AT + k], wd[k * TILE : (k + 1) * TILE, at])
        out_ref[:, at] = total.astype(bf16)

    tile_loop(o_tiles, feed_down)

    @pl.when(sec == 0)
    def _():
        forward_hop().start()

    out_copy = pltpu.make_async_copy(out_ref, out_hbm, o_sem.at[0])
    out_copy.start()

    @pl.when(rep == 0)
    def _():
        transpose_into(lt, 0, ab)

    @pl.when(rep == 1)
    def _():
        transpose_into(lt, 0, cb)

    @pl.when(sec == 0)
    def _():
        backward_hop().wait_recv()
        share_grad()

    def piece(v, j, t):
        alt = t % 3 == 2
        return jnp.where(alt, j % 2, v), jnp.where(alt, j // 2 * 2 + v, j)

    def product(t, v):
        tile = t // per_tile
        cols = pl.ds(pl.multiple_of(t % per_tile * CUT, CUT), CUT)
        h, r = lhs_of(rep, tile), rhs_of(rep, tile)
        places = [piece(v, j, t) for j in range(dp // 2)]
        mine = jnp.concatenate([lt[h, a, b] for a, b in places], axis=0)
        theirs = jnp.concatenate([ltr[h, a, b] for a, b in places], axis=0)
        return mul(mine, ra[r, :, cols]) + mul(theirs, rr[tile, :, cols])

    def open_tile(t):
        part_sum = product(t, 1 - half_of(0, t)).astype(bf16)
        for j in range(dp // 2):
            sends[0][t, j] = part_sum[j * shard : (j + 1) * shard]
        x_tile(0, t).start()

    def open_range(first, last):
        def run(t, carry):
            open_tile(t)
            return carry

        lax.fori_loop(first, last, run, 0)

    def merge(level, t):
        count = dp >> (level + 1)
        if level == 0:
            part_sum = product(t, half_of(0, t))
            x_tile(0, t).wait_recv()
            kept = [part_sum[j * shard : (j + 1) * shard] for j in range(count)]
        else:
            x_tile(level, t).wait_recv()
            kept = [sends[level][t, half_of(level, t), j].astype(f32) for j in range(count)]
        for j in range(count):
            total = (kept[j] + arrivals[level][t, j].astype(f32)).astype(bf16)
            if level + 1 < levels:
                sends[level + 1][t, j % 2, j // 2] = total
            else:
                ag[rep, t] = total
        if level + 1 < levels:
            x_tile(level + 1, t).start()
        else:
            g_tile(t).start()

    def feed_down_back(t, at, source, store, first):
        store[first + t] = (mul(source[...], wd[at, :], NT) * gp[:, at]).astype(bf16)

    tile_loop(u_tiles, partial(feed_down_back, source=eb, store=ra, first=U_AT))

    @pl.when(rep == 1)
    def _():
        y_act(0, cb).wait_recv()
        transpose_into(ltr, 0, pin.at[0])
        y_act(1, eb).wait_recv()
        transpose_into(ltr, 1, pin.at[1])

        def run(t, at):
            feed_up(t, at, pin.at[0], rr, 0)
            open_range(t * per_tile, (t + 1) * per_tile)

        tile_loop(u_tiles, run)

    def feed_up_back(t, at):
        total = mul(ra[U_AT], wu[at, 0:TILE], NT)
        for k in range(1, u_tiles):
            total = total + mul(ra[U_AT + k], wu[at, k * TILE : (k + 1) * TILE], NT)
        dcb[:, at] = total

    tile_loop(o_tiles, feed_up_back)

    def add_rows(i, value):
        acc[i] += jnp.sum(value.reshape(LN // 8, 8, width), axis=0)

    def second_back(at):
        d_c, normed = dcb[at], norm2[at]
        add_rows(1, d_c * normed)
        add_rows(3, d_c)
        d_m = eb[at].astype(f32) + normalize_back(d_c * gain_ref[0, 1:2], normed, inv2[at])
        mm[at] = d_m
        dmb[at] = d_m.astype(bf16)

    row_loop(second_back)

    @pl.when(rep == 1)
    def _():
        y_act(1, dmb).start()

    def attention_out_back(t, at, source):
        dob[:, at] = mul(source[...], wo[at, :], NT).astype(bf16)

    tile_loop(o_tiles, partial(attention_out_back, source=dmb))

    @pl.when(rep == 0)
    def _():
        transpose_into(lt, 1, dmb)

    def attend_back(pairs, store, first):
        def d_out(b, h):
            return dob[b * BLOCK : (b + 1) * BLOCK, pl.ds(pl.multiple_of(h * HEAD, HEAD), HEAD)]

        d_chances = [mul(d_out(b, h), part(b, 2, h), NT) for b, h in pairs]
        for b, h in pairs:
            store[tile_at(first + 2 * o_tiles, b, h)] = mul(probs[b, h].astype(bf16), d_out(b, h), TN).astype(bf16)
        d_scores = []
        for (b, h), d_probs in zip(pairs, d_chances):
            chance = probs[b, h]
            inner = jnp.sum(chance * d_probs, axis=-1, keepdims=True)
            d_scores.append((chance * (d_probs - inner)).astype(bf16))
        for (b, h), d_s in zip(pairs, d_scores):
            store[tile_at(first, b, h)] = (mul(d_s, part(b, 1, h)) * scale).astype(bf16)
        for (b, h), d_s in zip(pairs, d_scores):
            store[tile_at(first + o_tiles, b, h)] = (mul(d_s, part(b, 0, h), TN) * scale).astype(bf16)

    head_loop(partial(attend_back, store=ra, first=0))

    def project_back(t, at):
        total = mul(ra[0], wq[at, 0:TILE], NT)
        for k in range(1, q_tiles):
            total = total + mul(ra[k], wq[at, k * TILE : (k + 1) * TILE], NT)
        dcb[:, at] = total

    tile_loop(o_tiles, project_back)

    def first_back(at):
        d_a, normed = dcb[at], norm1[at]
        add_rows(0, d_a * normed)
        add_rows(2, d_a)
        d_h = mm[at] + normalize_back(d_a * gain_ref[0, 0:1], normed, inv1[at])
        dh_ref[at] = d_h.astype(bf16)

    row_loop(first_back)

    @pl.when(sec == 1)
    def _():
        backward_hop().start()

    dh_copy = pltpu.make_async_copy(dh_ref, dh_hbm, o_sem.at[1])
    dh_copy.start()

    @pl.when(rep == 0)
    def _():
        y_act(0, ab).wait_recv()
        transpose_into(ltr, 0, pin.at[0])
        y_act(1, dmb).wait_recv()
        transpose_into(ltr, 1, pin.at[1])
        for t in range(o_tiles):
            y_mixed(t).wait_recv()
        open_range(0, o_tiles * per_tile)
        project(lambda: pin[0])
        y_mask().wait_recv()
        head_loop(partial(chances_of, mask=mask2))
        tile_loop(o_tiles, partial(attention_out_back, source=pin.at[1]))
        head_loop(partial(attend_back, store=rr, first=o_tiles))

    @pl.when(rep == 1)
    def _():
        y_mask().wait_recv()
        tile_loop(u_tiles, partial(feed_down_back, source=pin.at[1], store=rr, first=u_tiles))


    for i in range(4):
        small[0, i : i + 1] = jnp.sum(acc[i], axis=0, keepdims=True)
        small[0, 4 + i : 5 + i] = jnp.zeros((1, width), f32)
    small_hop(0).start()

    def small_merge(n):
        small_hop(n).wait_recv()
        small[2 * n + 2] = small[2 * n] + small[2 * n + 1]
        if n < levels:
            small_hop(n + 1).start()

    lags = [2 + 3 * level for level in range(levels)]
    opened = jnp.where(rep == 0, o_tiles * per_tile, (u_tiles * per_tile))

    def reduce_step(s, carry):
        @pl.when(s + opened < cuts)
        def _():
            open_tile(s + opened)

        for level, lag in enumerate(lags):

            @pl.when((s >= lag) & (s < cuts + lag))
            def _():
                merge(level, s - lag)

        for n in range(levels + 1):

            @pl.when(s == 2 * n + 2)
            def _():
                small_merge(n)

        return carry

    lax.fori_loop(0, cuts + lags[-1], reduce_step, 0)

    if shard % 128 == 0:
        small_ref[...] = small[2 * levels + 2, :, pl.ds(pl.multiple_of(me * shard, shard), shard)]
    else:
        small_ref[...] = small[2 * levels + 2]

    def drain(t, carry):
        g_tile(t).wait_recv()
        for level in range(levels):
            x_tile(level, t).wait_send()
        g_tile(t).wait_send()
        return carry

    lax.fori_loop(0, cuts, drain, 0)
    grads_copy = pltpu.make_async_copy(ag, grad_hbm, o_sem.at[2])
    grads_copy.start()
    y_mask().wait_send()
    for h in range(2):
        y_act(h, eb).wait_send()

    @pl.when(rep == 1)
    def _():
        for t in range(o_tiles):
            y_mixed(t).wait_send()

    for n in range(levels + 1):
        small_hop(n).wait_send()

    @pl.when(sec == 0)
    def _():
        forward_hop().wait_send()

    @pl.when(sec == 1)
    def _():
        backward_hop().wait_send()

    out_copy.wait()
    dh_copy.wait()
    grads_copy.wait()


def finish_kernel(near, turn, grad_ref, out_ref, dh_ref, gq, go, gu, gd, out, dh):
    t = pl.program_id(0)

    for r, first, second in ((0, go, gq), (1, gd, gu)):
        for c in range(grad_ref.shape[1]):
            at = slice(c * CUT, (c + 1) * CUT)

            @pl.when(t < near[r])
            def _():
                if turn:
                    first[0, at, :] = grad_ref[r, c].T.astype(f32)
                else:
                    first[0, :, at] = grad_ref[r, c].astype(f32)

            @pl.when(t >= near[r])
            def _():
                second[0, :, at] = grad_ref[r, c].astype(f32)

    out[0] = out_ref[...]
    dh[0] = dh_ref[...]


def per_device(inputs, cotangent, seg_counts, w_qkv, w_out, w_up, w_down, gains, biases):
    dp = lax.axis_size("dp")
    levels = dp.bit_length() - 1
    rows, width = inputs.shape
    ff = w_up.shape[2]
    shard = width // dp
    whole_lanes = shard % 128 == 0
    tiles = 2 * ff // TILE
    cuts = tiles * TILE // CUT
    q_tiles, o_tiles, u_tiles = 3 * width // TILE, width // TILE, ff // TILE
    blocks, heads = rows // BLOCK, width // HEAD
    dma = pltpu.SemaphoreType.DMA
    vm = pltpu.VMEM
    act = vm((rows, width), bf16)
    wide = vm((rows, width), f32)
    scratch = [
        vm((width, 3 * width), bf16), vm((width, width), bf16), vm((width, ff), bf16), vm((ff, width), bf16),
        act, act, wide, wide, vm((rows, 1), f32), vm((rows, 1), f32),
        act, vm((rows, 3 * width), bf16), act, act, act,
        vm((blocks, heads, BLOCK, BLOCK), f32), wide, vm((rows, ff), f32), wide,
        vm((4, 8, width), f32), vm((blocks, BLOCK, BLOCK), f32),
        vm((blocks, BLOCK, BLOCK), f32), vm((2, rows, width), bf16),
        act, act,
        vm((2, 2, dp // 2, shard, rows), bf16),
        vm((2, 2, dp // 2, shard, rows), bf16),
        vm((2 * tiles, rows, TILE), bf16),
        vm((tiles, rows, TILE), bf16),
        vm((2, cuts, shard, CUT), bf16),
        vm((2 * levels + 3, 8, width), f32),
        vm((cuts, dp // 2, shard, CUT), bf16),
        *[vm((cuts, 2, dp >> (level + 1), shard, CUT), bf16) for level in range(1, levels)],
        *[vm((cuts, dp >> (level + 1), shard, CUT), bf16) for level in range(levels)],
        dma((4,)), dma((4,)),
        dma((3 + o_tiles,)), dma((3 + o_tiles,)),
        dma((levels, cuts)), dma((levels, cuts)),
        dma((cuts,)), dma((cuts,)),
        dma((levels + 1,)), dma((levels + 1,)),
        dma((2,)), dma((2,)),
    ]
    vspec = pl.BlockSpec(memory_space=pltpu.VMEM)
    hbm = pl.BlockSpec(memory_space=pl.ANY)
    sds = jax.ShapeDtypeStruct
    out, d_h, grads, small = pl.pallas_call(
        step_kernel,
        out_shape=(
            sds((rows, width), bf16), sds((rows, width), bf16),
            sds((2, cuts, shard, CUT), bf16),
            sds((8, shard if whole_lanes else width), f32),
        ),
        in_specs=[hbm, hbm, pl.BlockSpec(memory_space=pltpu.SMEM)] + [hbm] * 4 + [vspec] * 2,
        out_specs=(hbm, hbm, hbm, vspec),
        scratch_shapes=scratch,
        name="layers_step",
        compiler_params=pltpu.CompilerParams(
            collective_id=0, has_side_effects=True, vmem_limit_bytes=67043328
        ),
    )(inputs, cotangent, seg_counts, w_qkv, w_out, w_up, w_down, gains, biases)

    def turned(n, near):
        if whole_lanes:
            return sds((1, n, shard), f32), pl.BlockSpec((1, width, shard), lambda t: (0, jnp.minimum(t, near - 1), 0))
        return sds((1, shard, n), f32), pl.BlockSpec((1, shard, width), lambda t: (0, 0, jnp.minimum(t, near - 1)))

    def flat(n, near):
        return sds((1, shard, n), f32), pl.BlockSpec((1, shard, width), lambda t: (0, 0, jnp.maximum(t - near, 0)))

    steps = 2 * ff // width
    near = (1, ff // width)
    step = rows // steps
    copied = sds((1, rows, width), bf16), pl.BlockSpec((1, step, width), lambda t: (0, t, 0))
    shapes = (flat(3 * width, near[0]), turned(width, near[0]), flat(ff, near[1]), turned(ff, near[1]), copied, copied)
    by_rows = pl.BlockSpec((step, width), lambda t: (t, 0))
    g_q, g_o, g_u, g_d, out, d_h = pl.pallas_call(
        partial(finish_kernel, near, whole_lanes),
        grid=(steps,),
        out_shape=[shape for shape, _ in shapes],
        in_specs=[pl.BlockSpec((2, cuts // steps, shard, CUT), lambda t: (0, t, 0, 0)), by_rows, by_rows],
        out_specs=[spec for _, spec in shapes],
        name="finish",
    )(grads, out, d_h)
    if not whole_lanes:
        g_o, g_d = jnp.swapaxes(g_o, 1, 2), jnp.swapaxes(g_d, 1, 2)
        small = lax.dynamic_slice_in_dim(small, lax.axis_index("dp") * shard, shard, 1)
    return (out, d_h, g_q, g_o, g_u, g_d, small[None, 0:2], small[None, 2:4])


def solution(mesh):
    rows = P(("dp", "rep"), None)
    layer = P("section", None, None)
    return jax.shard_map(
        per_device,
        mesh=mesh,
        in_specs=(rows, rows, P(("dp", "rep"))) + (layer,) * 6,
        out_specs=(
            P("section", ("dp", "rep"), None),
            P("section", ("dp", "rep"), None),
            P("section", "dp", None),
            P("section", None, "dp"),
            P("section", "dp", None),
            P("section", None, "dp"),
            P("section", None, "dp"),
            P("section", None, "dp"),
        ),
        check_vma=False,
    )
```

time: 189 us -> 153 us (0.81)
  Pallas kernels: 179 us -> 151 us
  other arithmetic: 6.41 us -> 0 us
    pallas_call x1 -> x2, Pallas kernels: 179 us -> 151 us  [the longest x1 146 us: per_device(): pl.pallas_call(step_kernel, out_shape=(sds((rows, width), bf16), sds((row...]
    broadcast_in_dim x4 -> x0, other arithmetic: 6.41 us -> none  [per_device(): grads = [g.astype(f32)[None] for g in (g_q, g_o, g_u, g_d)]]
where the time goes in v1:
time: 153 us
  Pallas kernels  151 us (99%)
    pallas_call x1, Pallas kernels, per_device(): pl.pallas_call(step_kernel, out_shape=(sds((rows, width), bf16), sds((row...  146 us
    pallas_call x1, Pallas kernels, per_device(): pl.pallas_call(partial(finish_kernel, near, whole_lanes), grid=(steps,),...  5.27 us

profile of v1, /device:TPU:0, one launch (start us, length us, event | category | flops | bytes accessed | tf_op | source)
XLA Modules:
  0.0 152.9 jit_solution(1960132511943985025)
XLA Ops:
  0.6 145.7 %layers_step.1 = (bf16[256,1024]{1,0:T(8,128)(2,1)}, bf16[256,1024]{1,0:T(8,128)(2,1)}, bf16[2,16,128,256]{3,2,1,0:T(8,128)(2,1)}, f32[8,128]{1,0:T(8,128)}) custom-call(bf16[256,1024]{1,0:T(8,128)(2,1)} %x_hbm.1, bf16[256,1024]{1,0:T(8,128)(2,1)} %ct_hbm.1, s32[16]{0:T(128)} %count_ref.1, bf16[1,1024,3072]{2,1,0:T(8,128)(2,1)} %wq_hbm.1, ...), custom_call_target="tpu_custom_call" | custom-call | tf_op jit(solution)/shard_map/layers_step/pallas_call | solution.py:640
  146.3 1.3 slice_bitcast_fusion
  147.6 5.3 %finish.1 = (f32[1,128,3072]{2,1,0:T(8,128)}, f32[1,1024,128]{2,1,0:T(8,128)}, f32[1,128,2048]{2,1,0:T(8,128)}, f32[1,2048,128]{2,1,0:T(8,128)}, bf16[1,256,1024...) custom-call(bf16[2,16,128,256]{3,2,1,0:T(8,128)(2,1)} %get-tuple-element.18.grad_ref, ...), custom_call_target="tpu_custom_call" | custom-call | tf_op jit(solution)/shard_map/finish/pallas_call | solution.py:670

commit v2 on v1

--- a/solution.py
+++ b/solution.py
@@ -96,22 +96,25 @@
         copy.start()
 
     barrier = pltpu.get_barrier_semaphore()
-    peers = [s_to, y_to] + [x_to(bit) for bit in range(levels)]
+    peers = [s_to, y_to, (1 - sec, me, other)] + [x_to(bit) for bit in range(levels)]
     for peer in peers:
         pl.semaphore_signal(barrier, inc=1, device_id=peer, device_id_type=MESH)
     pl.semaphore_wait(barrier, len(peers))
 
     q_tiles, o_tiles, u_tiles = 3 * width // TILE, width // TILE, ff // TILE
     O_AT, U_AT, G_AT = q_tiles, tiles, tiles + u_tiles
-
-    def early(r):
-        return jnp.where(r == 0, o_tiles, u_tiles)
-
-    def rhs_of(r, t):
-        return r * tiles + (t + tiles - early(r)) % tiles
-
-    def lhs_of(r, t):
-        return jnp.where(t < early(r), 1, 0)
+    o_half, u_half = o_tiles // 2, u_tiles // 2
+    UP, OUT, QKV = u_half, 2 * u_half, 2 * u_half + o_half
+    A, DM, C, E = range(4)
+
+    def own_tile(t):
+        k = t - QKV
+        at = jnp.where(t < OUT, U_AT + rep * u_half + t - UP, O_AT + rep * o_half + t - OUT)
+        at = jnp.where(t < UP, G_AT + rep * u_half + t, at)
+        return jnp.where(t < QKV, at, k // o_half * o_tiles + rep * o_half + k % o_half)
+
+    def side_of(t):
+        return jnp.where(t < UP, E, jnp.where(t < OUT, C, jnp.where(t < QKV, DM, A)))
 
     def remote(src, dst, ss, rs, to):
         return pltpu.make_async_remote_copy(
@@ -127,14 +130,14 @@
     def y_hop(n, src, dst):
         return remote(src, dst, y_send.at[n], y_recv.at[n], y_to)
 
-    def y_act(h, src):
-        return y_hop(h, src, pin.at[h])
+    def y_act(n, src):
+        return y_hop(n, src, pin.at[n])
+
+    def cross_hop():
+        return remote(dh_ref, pin.at[E], p_send.at[2], y_recv.at[E], (1 - sec, me, other))
 
     def y_mask():
-        return y_hop(2, mask, mask2)
-
-    def y_mixed(t):
-        return y_hop(3 + t, ra.at[O_AT + t], rr.at[t])
+        return y_hop(4, mask, mask2)
 
     def bit_of(level, t):
         return jnp.where(t % 3 == 2, 1 - level, level) if level < 2 else level
@@ -156,7 +159,7 @@
         return remote(ag.at[rep, t], ag.at[rep, t], g_send.at[t], g_recv.at[t], y_to)
 
     def small_hop(n):
-        to = x_to(n) if n < levels else y_to
+        to = x_to(levels - n) if n else y_to
         return remote(small.at[2 * n], small.at[2 * n + 1], s_send.at[n], s_recv.at[n], to)
 
     def transpose_into(lt, m, ref):
@@ -199,13 +202,8 @@
     y_mask().start()
 
     def share_grad():
-        @pl.when(rep == 0)
-        def _():
-            y_act(1, eb).start()
-
-        @pl.when(rep == 1)
-        def _():
-            transpose_into(lt, 1, eb)
+        y_act(E, eb).start()
+        transpose_into(lt, E, eb)
 
     @pl.when(sec == 0)
     def _():
@@ -225,26 +223,19 @@
 
     row_loop(first_norm)
 
-    @pl.when(rep == 1)
-    def _():
-        y_act(0, ab).start()
-
+    y_act(A, ab).start()
     weights[0].wait()
 
-    def project(source):
-        def run(t, at):
-            pb[:, at] = mul(source(), wq[:, at]).astype(bf16)
-
-        tile_loop(q_tiles, run)
-
-    project(lambda: ab[...])
-
-    def head_loop(body):
-        def run(i, carry):
-            body([(b, i * 8 + u) for u in range(8) for b in range(blocks)])
-            return carry
-
-        lax.fori_loop(0, heads // 8, run, 0)
+    def cols_of(t):
+        return pl.ds(pl.multiple_of(t * TILE, TILE), TILE)
+
+    def project(t, at):
+        pb[:, at] = mul(ab[...], wq[:, at]).astype(bf16)
+
+    tile_loop(q_tiles, project)
+
+    def pairs_of(first, count):
+        return [(b, first + u, u) for u in range(count) for b in range(blocks)]
 
     def part(b, member, h):
         return pb[b * BLOCK : (b + 1) * BLOCK, pl.ds(pl.multiple_of(member * width + h * HEAD, HEAD), HEAD)]
@@ -255,9 +246,9 @@
         return (first + h // group, pl.ds(b * BLOCK, BLOCK), cols)
 
     def chances_of(pairs, mask):
-        scores = [mul(part(b, 0, h), part(b, 1, h), NT) for b, h in pairs]
+        scores = [mul(part(b, 0, h), part(b, 1, h), NT) for b, h, _ in pairs]
         chances = []
-        for (b, h), score in zip(pairs, scores):
+        for (b, h, _), score in zip(pairs, scores):
             score = jnp.where(mask[b] > 0.5, score * scale, -1e30)
             raised = jnp.exp(score - jnp.max(score, axis=-1, keepdims=True))
             chance = raised * (1.0 / jnp.sum(raised, axis=-1, keepdims=True))
@@ -265,17 +256,11 @@
             chances.append(chance.astype(bf16))
         return chances
 
-    def attend(pairs):
-        for (b, h), chance in zip(pairs, chances_of(pairs, mask)):
-            ra[tile_at(O_AT, b, h)] = mul(chance, part(b, 2, h)).astype(bf16)
-
-    head_loop(attend)
-
-    @pl.when(rep == 1)
-    def _():
-        for t in range(o_tiles):
-            y_mixed(t).start()
-
+    def attend(pairs, mask, store, first):
+        for (b, h, u), chance in zip(pairs, chances_of(pairs, mask)):
+            store[tile_at(first, b, u)] = mul(chance, part(b, 2, h)).astype(bf16)
+
+    attend(pairs_of(0, heads), mask, ra, O_AT)
     weights[1].wait()
 
     def attention_out(t, at):
@@ -294,10 +279,7 @@
 
     row_loop(second_norm)
 
-    @pl.when(rep == 0)
-    def _():
-        y_act(0, cb).start()
-
+    y_act(C, cb).start()
     weights[2].wait()
 
     def feed_up(t, at, source, store, first):
@@ -323,18 +305,23 @@
     out_copy = pltpu.make_async_copy(out_ref, out_hbm, o_sem.at[0])
     out_copy.start()
 
-    @pl.when(rep == 0)
-    def _():
-        transpose_into(lt, 0, ab)
-
-    @pl.when(rep == 1)
-    def _():
-        transpose_into(lt, 0, cb)
+    transpose_into(lt, C, cb)
+    transpose_into(lt, A, ab)
+
+    def meet_c():
+        y_act(C, cb).wait_recv()
+        transpose_into(ltr, C, pin.at[C])
+
+    def meet_a():
+        y_act(A, ab).wait_recv()
+        transpose_into(ltr, A, pin.at[A])
 
     @pl.when(sec == 0)
     def _():
+        meet_c()
+        meet_a()
         backward_hop().wait_recv()
-        share_grad()
+        transpose_into(lt, E, eb)
 
     def piece(v, j, t):
         alt = t % 3 == 2
@@ -343,7 +330,7 @@
     def product(t, v):
         tile = t // per_tile
         cols = pl.ds(pl.multiple_of(t % per_tile * CUT, CUT), CUT)
-        h, r = lhs_of(rep, tile), rhs_of(rep, tile)
+        h, r = side_of(tile), own_tile(tile)
         places = [piece(v, j, t) for j in range(dp // 2)]
         mine = jnp.concatenate([lt[h, a, b] for a, b in places], axis=0)
         theirs = jnp.concatenate([ltr[h, a, b] for a, b in places], axis=0)
@@ -382,23 +369,34 @@
         else:
             g_tile(t).start()
 
+    def merge_range(first, last):
+        def run(t, carry):
+            merge(0, t)
+            return carry
+
+        lax.fori_loop(first, last, run, 0)
+
+    def on(section, run):
+        pl.when(sec == section)(run)
+
     def feed_down_back(t, at, source, store, first):
         store[first + t] = (mul(source[...], wd[at, :], NT) * gp[:, at]).astype(bf16)
 
     tile_loop(u_tiles, partial(feed_down_back, source=eb, store=ra, first=U_AT))
 
-    @pl.when(rep == 1)
-    def _():
-        y_act(0, cb).wait_recv()
-        transpose_into(ltr, 0, pin.at[0])
-        y_act(1, eb).wait_recv()
-        transpose_into(ltr, 1, pin.at[1])
-
-        def run(t, at):
-            feed_up(t, at, pin.at[0], rr, 0)
-            open_range(t * per_tile, (t + 1) * per_tile)
-
-        tile_loop(u_tiles, run)
+    def half_up(t, _):
+        feed_up(t, cols_of(rep * u_half + t), pin.at[C], rr, 0)
+        open_range(t * per_tile, (t + 1) * per_tile)
+
+    def half_down_back(t, _):
+        feed_down_back(t, cols_of(rep * u_half + t), pin.at[E], rr, UP)
+        open_range((UP + t) * per_tile, (UP + t + 1) * per_tile)
+
+    def feed_half():
+        on(1, meet_c)
+        y_act(E, eb).wait_recv()
+        transpose_into(ltr, E, pin.at[E])
+        tile_loop(u_half, half_up)
 
     def feed_up_back(t, at):
         total = mul(ra[U_AT], wu[at, 0:TILE], NT)
@@ -421,45 +419,41 @@
 
     row_loop(second_back)
 
-    @pl.when(rep == 1)
-    def _():
-        y_act(1, dmb).start()
+    y_act(DM, dmb).start()
+    on(1, feed_half)
 
     def attention_out_back(t, at, source):
         dob[:, at] = mul(source[...], wo[at, :], NT).astype(bf16)
 
     tile_loop(o_tiles, partial(attention_out_back, source=dmb))
 
-    @pl.when(rep == 0)
-    def _():
-        transpose_into(lt, 1, dmb)
-
-    def attend_back(pairs, store, first):
+    transpose_into(lt, DM, dmb)
+
+    def attend_back(pairs, store, first, stride):
         def d_out(b, h):
             return dob[b * BLOCK : (b + 1) * BLOCK, pl.ds(pl.multiple_of(h * HEAD, HEAD), HEAD)]
 
-        d_chances = [mul(d_out(b, h), part(b, 2, h), NT) for b, h in pairs]
-        for b, h in pairs:
-            store[tile_at(first + 2 * o_tiles, b, h)] = mul(probs[b, h].astype(bf16), d_out(b, h), TN).astype(bf16)
+        d_chances = [mul(d_out(b, h), part(b, 2, h), NT) for b, h, _ in pairs]
+        for b, h, u in pairs:
+            d_v = mul(probs[b, h].astype(bf16), d_out(b, h), TN)
+            store[tile_at(first + 2 * stride, b, u)] = d_v.astype(bf16)
         d_scores = []
-        for (b, h), d_probs in zip(pairs, d_chances):
+        for (b, h, _), d_probs in zip(pairs, d_chances):
             chance = probs[b, h]
             inner = jnp.sum(chance * d_probs, axis=-1, keepdims=True)
             d_scores.append((chance * (d_probs - inner)).astype(bf16))
-        for (b, h), d_s in zip(pairs, d_scores):
-            store[tile_at(first, b, h)] = (mul(d_s, part(b, 1, h)) * scale).astype(bf16)
-        for (b, h), d_s in zip(pairs, d_scores):
-            store[tile_at(first + o_tiles, b, h)] = (mul(d_s, part(b, 0, h), TN) * scale).astype(bf16)
-
-    head_loop(partial(attend_back, store=ra, first=0))
+        for (b, h, u), d_s in zip(pairs, d_scores):
+            store[tile_at(first, b, u)] = (mul(d_s, part(b, 1, h)) * scale).astype(bf16)
+        for (b, h, u), d_s in zip(pairs, d_scores):
+            store[tile_at(first + stride, b, u)] = (mul(d_s, part(b, 0, h), TN) * scale).astype(bf16)
+
+    attend_back(pairs_of(0, heads), ra, 0, o_tiles)
 
     def project_back(t, at):
         total = mul(ra[0], wq[at, 0:TILE], NT)
         for k in range(1, q_tiles):
             total = total + mul(ra[k], wq[at, k * TILE : (k + 1) * TILE], NT)
         dcb[:, at] = total
-
-    tile_loop(o_tiles, project_back)
 
     def first_back(at):
         d_a, normed = dcb[at], norm1[at]
@@ -468,35 +462,46 @@
         d_h = mm[at] + normalize_back(d_a * gain_ref[0, 0:1], normed, inv1[at])
         dh_ref[at] = d_h.astype(bf16)
 
-    row_loop(first_back)
+    dh_copy = pltpu.make_async_copy(dh_ref, dh_hbm, o_sem.at[1])
+
+    def input_back():
+        tile_loop(o_tiles, project_back)
+        row_loop(first_back)
+        dh_copy.start()
 
     @pl.when(sec == 1)
     def _():
+        input_back()
         backward_hop().start()
-
-    dh_copy = pltpu.make_async_copy(dh_ref, dh_hbm, o_sem.at[1])
-    dh_copy.start()
-
-    @pl.when(rep == 0)
-    def _():
-        y_act(0, ab).wait_recv()
-        transpose_into(ltr, 0, pin.at[0])
-        y_act(1, dmb).wait_recv()
-        transpose_into(ltr, 1, pin.at[1])
-        for t in range(o_tiles):
-            y_mixed(t).wait_recv()
-        open_range(0, o_tiles * per_tile)
-        project(lambda: pin[0])
-        y_mask().wait_recv()
-        head_loop(partial(chances_of, mask=mask2))
-        tile_loop(o_tiles, partial(attention_out_back, source=pin.at[1]))
-        head_loop(partial(attend_back, store=rr, first=o_tiles))
-
-    @pl.when(rep == 1)
-    def _():
-        y_mask().wait_recv()
-        tile_loop(u_tiles, partial(feed_down_back, source=pin.at[1], store=rr, first=u_tiles))
-
+        cross_hop().start()
+        meet_a()
+
+    @pl.when(sec == 0)
+    def _():
+        input_back()
+        feed_half()
+
+    tile_loop(u_half, half_down_back)
+    merge_range(0, 4)
+
+    def half_project(t, _):
+        at = cols_of(t // o_half * o_tiles + rep * o_half + t % o_half)
+        pb[:, at] = mul(pin[A], wq[:, at]).astype(bf16)
+
+    tile_loop(3 * o_half, half_project)
+    y_mask().wait_recv()
+    half = pairs_of(rep * (heads // 2), heads // 2)
+    attend(half, mask2, rr, OUT)
+    y_act(DM, dmb).wait_recv()
+    transpose_into(ltr, DM, pin.at[DM])
+    open_range(OUT * per_tile, QKV * per_tile)
+    merge_range(4, 6)
+
+    def half_out_back(t, _):
+        attention_out_back(t, cols_of(rep * o_half + t), pin.at[DM])
+
+    tile_loop(o_half, half_out_back)
+    attend_back(half, rr, QKV, o_half)
 
     for i in range(4):
         small[0, i : i + 1] = jnp.sum(acc[i], axis=0, keepdims=True)
@@ -509,15 +514,19 @@
         if n < levels:
             small_hop(n + 1).start()
 
-    lags = [2 + 3 * level for level in range(levels)]
-    opened = jnp.where(rep == 0, o_tiles * per_tile, (u_tiles * per_tile))
+    lags = [3 * level - 3 for level in range(levels)]
+    opened = QKV * per_tile
 
     def reduce_step(s, carry):
         @pl.when(s + opened < cuts)
         def _():
             open_tile(s + opened)
 
-        for level, lag in enumerate(lags):
+        @pl.when(s + 6 < cuts)
+        def _():
+            merge(0, s + 6)
+
+        for level, lag in enumerate(lags[1:], 1):
 
             @pl.when((s >= lag) & (s < cuts + lag))
             def _():
@@ -525,7 +534,7 @@
 
         for n in range(levels + 1):
 
-            @pl.when(s == 2 * n + 2)
+            @pl.when(s == 4 * n + 3)
             def _():
                 small_merge(n)
 
@@ -549,13 +558,8 @@
     grads_copy = pltpu.make_async_copy(ag, grad_hbm, o_sem.at[2])
     grads_copy.start()
     y_mask().wait_send()
-    for h in range(2):
-        y_act(h, eb).wait_send()
-
-    @pl.when(rep == 1)
-    def _():
-        for t in range(o_tiles):
-            y_mixed(t).wait_send()
+    for n in (A, DM, C):
+        y_act(n, ab).wait_send()
 
     for n in range(levels + 1):
         small_hop(n).wait_send()
@@ -567,32 +571,72 @@
     @pl.when(sec == 1)
     def _():
         backward_hop().wait_send()
+        cross_hop().wait_send()
+        y_act(E, eb).wait_send()
 
     out_copy.wait()
     dh_copy.wait()
     grads_copy.wait()
 
 
-def finish_kernel(near, turn, grad_ref, out_ref, dh_ref, gq, go, gu, gd, out, dh):
-    t = pl.program_id(0)
-
-    for r, first, second in ((0, go, gq), (1, gd, gu)):
-        for c in range(grad_ref.shape[1]):
-            at = slice(c * CUT, (c + 1) * CUT)
-
-            @pl.when(t < near[r])
-            def _():
-                if turn:
-                    first[0, at, :] = grad_ref[r, c].T.astype(f32)
-                else:
-                    first[0, :, at] = grad_ref[r, c].astype(f32)
-
-            @pl.when(t >= near[r])
-            def _():
-                second[0, :, at] = grad_ref[r, c].astype(f32)
-
-    out[0] = out_ref[...]
-    dh[0] = dh_ref[...]
+def finish_kernel(
+    turn, grad_hbm, out_hbm, dh_hbm, small_ref, gq_hbm, go_hbm, gu_hbm, gd_hbm, out_to, dh_to, gain_ref, bias_ref,
+    raw, kept, q, o, u, d, in_sem, out_sem,
+):
+    cuts, width, ff = raw.shape[1], kept.shape[2], u.shape[1]
+    gain_ref[0] = small_ref[0:2]
+    bias_ref[0] = small_ref[2:4]
+    quarter = ff // 2 // CUT
+    sizes = (quarter, quarter, width // 2 // CUT, 3 * width // 2 // CUT)
+    copies = [(out_hbm, out_to), (dh_hbm, dh_to)]
+    loads = []
+    for n, (source, _) in enumerate(copies):
+        loads.append(pltpu.make_async_copy(source, kept.at[n], in_sem.at[n]))
+    for r in range(2):
+        first = 0
+        for size in sizes:
+            at = pl.ds(first, size)
+            loads.append(pltpu.make_async_copy(grad_hbm.at[r, at], raw.at[r, at], in_sem.at[len(loads)]))
+            first += size
+    for load in loads:
+        load.start()
+    stores = []
+
+    def store(source, target):
+        stores.append(pltpu.make_async_copy(source, target, out_sem.at[len(stores)]))
+        stores[-1].start()
+
+    def place(buffer, target, turned, r, first, count, at):
+        for c in range(count):
+            piece = raw[r, first + c]
+            cols = slice(at + c * CUT, at + (c + 1) * CUT)
+            if turned and turn:
+                buffer[cols, :] = piece.astype(f32).T
+            else:
+                buffer[:, cols] = piece.astype(f32)
+        size = count * CUT
+        if turned and turn:
+            store(buffer.at[pl.ds(at, size)], target.at[0, pl.ds(at, size)])
+        else:
+            store(buffer.at[:, pl.ds(at, size)], target.at[0, :, pl.ds(at, size)])
+
+    for n, (_, target) in enumerate(copies):
+        loads[n].wait()
+        store(kept.at[n], target.at[0])
+    n = 2
+    for r in range(2):
+        first = 0
+        for size, (buffer, target, turned) in zip(sizes, ((d, gd_hbm, True), (u, gu_hbm, False), (o, go_hbm, True), (q, gq_hbm, False))):
+            loads[n].wait()
+            n += 1
+            if buffer is q:
+                for m in range(3):
+                    place(buffer, target, turned, r, first + m * (size // 3), size // 3, m * width + r * (width // 2))
+            else:
+                place(buffer, target, turned, r, first, size, r * size * CUT)
+            first += size
+    for copy in stores:
+        copy.wait()
 
 
 def per_device(inputs, cotangent, seg_counts, w_qkv, w_out, w_up, w_down, gains, biases):
@@ -616,10 +660,10 @@
         act, vm((rows, 3 * width), bf16), act, act, act,
         vm((blocks, heads, BLOCK, BLOCK), f32), wide, vm((rows, ff), f32), wide,
         vm((4, 8, width), f32), vm((blocks, BLOCK, BLOCK), f32),
-        vm((blocks, BLOCK, BLOCK), f32), vm((2, rows, width), bf16),
+        vm((blocks, BLOCK, BLOCK), f32), vm((4, rows, width), bf16),
         act, act,
-        vm((2, 2, dp // 2, shard, rows), bf16),
-        vm((2, 2, dp // 2, shard, rows), bf16),
+        vm((4, 2, dp // 2, shard, rows), bf16),
+        vm((4, 2, dp // 2, shard, rows), bf16),
         vm((2 * tiles, rows, TILE), bf16),
         vm((tiles, rows, TILE), bf16),
         vm((2, cuts, shard, CUT), bf16),
@@ -628,11 +672,11 @@
         *[vm((cuts, 2, dp >> (level + 1), shard, CUT), bf16) for level in range(1, levels)],
         *[vm((cuts, dp >> (level + 1), shard, CUT), bf16) for level in range(levels)],
         dma((4,)), dma((4,)),
-        dma((3 + o_tiles,)), dma((3 + o_tiles,)),
+        dma((5,)), dma((5,)),
         dma((levels, cuts)), dma((levels, cuts)),
         dma((cuts,)), dma((cuts,)),
         dma((levels + 1,)), dma((levels + 1,)),
-        dma((2,)), dma((2,)),
+        dma((3,)), dma((2,)),
     ]
     vspec = pl.BlockSpec(memory_space=pltpu.VMEM)
     hbm = pl.BlockSpec(memory_space=pl.ANY)
@@ -653,32 +697,29 @@
         ),
     )(inputs, cotangent, seg_counts, w_qkv, w_out, w_up, w_down, gains, biases)
 
-    def turned(n, near):
-        if whole_lanes:
-            return sds((1, n, shard), f32), pl.BlockSpec((1, width, shard), lambda t: (0, jnp.minimum(t, near - 1), 0))
-        return sds((1, shard, n), f32), pl.BlockSpec((1, shard, width), lambda t: (0, 0, jnp.minimum(t, near - 1)))
-
-    def flat(n, near):
-        return sds((1, shard, n), f32), pl.BlockSpec((1, shard, width), lambda t: (0, 0, jnp.maximum(t - near, 0)))
-
-    steps = 2 * ff // width
-    near = (1, ff // width)
-    step = rows // steps
-    copied = sds((1, rows, width), bf16), pl.BlockSpec((1, step, width), lambda t: (0, t, 0))
-    shapes = (flat(3 * width, near[0]), turned(width, near[0]), flat(ff, near[1]), turned(ff, near[1]), copied, copied)
-    by_rows = pl.BlockSpec((step, width), lambda t: (t, 0))
-    g_q, g_o, g_u, g_d, out, d_h = pl.pallas_call(
-        partial(finish_kernel, near, whole_lanes),
-        grid=(steps,),
-        out_shape=[shape for shape, _ in shapes],
-        in_specs=[pl.BlockSpec((2, cuts // steps, shard, CUT), lambda t: (0, t, 0, 0)), by_rows, by_rows],
-        out_specs=[spec for _, spec in shapes],
+    def shaped(n, turn):
+        return (n, shard) if turn and whole_lanes else (shard, n)
+
+    if not whole_lanes:
+        small = lax.dynamic_slice_in_dim(small, lax.axis_index("dp") * shard, shard, 1)
+    ends = ((3 * width, False), (width, True), (ff, False), (ff, True))
+    g_q, g_o, g_u, g_d, out, d_h, gain_grads, bias_grads = pl.pallas_call(
+        partial(finish_kernel, whole_lanes),
+        out_shape=[sds((1, *shaped(n, turn)), f32) for n, turn in ends]
+        + [sds((1, rows, width), bf16)] * 2
+        + [sds((1, 2, shard), f32)] * 2,
+        in_specs=[hbm, hbm, hbm, vspec],
+        out_specs=[hbm] * 6 + [vspec] * 2,
+        scratch_shapes=[
+            vm((2, cuts, shard, CUT), bf16), vm((2, rows, width), bf16),
+            *[vm(shaped(n, turn), f32) for n, turn in ends],
+            dma((10,)), dma((16,)),
+        ],
         name="finish",
-    )(grads, out, d_h)
+    )(grads, out, d_h, small)
     if not whole_lanes:
         g_o, g_d = jnp.swapaxes(g_o, 1, 2), jnp.swapaxes(g_d, 1, 2)
-        small = lax.dynamic_slice_in_dim(small, lax.axis_index("dp") * shard, shard, 1)
-    return (out, d_h, g_q, g_o, g_u, g_d, small[None, 0:2], small[None, 2:4])
+    return (out, d_h, g_q, g_o, g_u, g_d, gain_grads, bias_grads)
 
 
 def solution(mesh):

time: 153 us -> 145 us (0.948)
  Pallas kernels: 151 us -> 144 us
    pallas_call x1, Pallas kernels: 146 us -> 139 us  [per_device(): pl.pallas_call(step_kernel, out_shape=(sds((rows, width), bf16), sds((row...]
where the time goes in v2:
time: 145 us
  Pallas kernels  144 us (99%)
    pallas_call x1, Pallas kernels, per_device(): pl.pallas_call(step_kernel, out_shape=(sds((rows, width), bf16), sds((row...  139 us
    pallas_call x1, Pallas kernels, per_device(): pl.pallas_call(partial(finish_kernel, whole_lanes), out_shape=[sds((1, *s...  4.85 us

profile of v2, /device:TPU:0, one launch (start us, length us, event | category | flops | bytes accessed | tf_op | source)
XLA Modules:
  0.0 144.6 jit_solution(8034544346829288951)
XLA Ops:
  0.6 138.9 %layers_step.1 = (bf16[256,1024]{1,0:T(8,128)(2,1)}, bf16[256,1024]{1,0:T(8,128)(2,1)}, bf16[2,16,128,256]{3,2,1,0:T(8,128)(2,1)}, f32[8,128]{1,0:T(8,128)}) custom-call(bf16[256,1024]{1,0:T(8,128)(2,1)} %x_hbm.1, bf16[256,1024]{1,0:T(8,128)(2,1)} %ct_hbm.1, s32[16]{0:T(128)} %count_ref.1, bf16[1,1024,3072]{2,1,0:T(8,128)(2,1)} %wq_hbm.1, ...), custom_call_target="tpu_custom_call" | custom-call | tf_op jit(solution)/shard_map/layers_step/pallas_call | solution.py:684
  139.6 4.9 %finish.1 = (f32[1,128,3072]{2,1,0:T(8,128)}, f32[1,1024,128]{2,1,0:T(8,128)}, f32[1,128,2048]{2,1,0:T(8,128)}, f32[1,2048,128]{2,1,0:T(8,128)}, bf16[1,256,1024...) custom-call(bf16[2,16,128,256]{3,2,1,0:T(8,128)(2,1)} %get-tuple-element.20.grad_hb, ...), custom_call_target="tpu_custom_call" | custom-call | tf_op jit(solution)/shard_map/finish/pallas_call | solution.py:706

commit v3 on v2

--- a/solution.py
+++ b/solution.py
@@ -79,8 +79,12 @@
 
     weights = [
         pltpu.make_async_copy(src.at[0], dst, w_sem.at[i])
-        for i, (src, dst) in enumerate(((wq_hbm, wq), (wo_hbm, wo), (wu_hbm, wu), (wd_hbm, wd)))
+        for i, (src, dst) in enumerate(((wo_hbm, wo), (wu_hbm, wu), (wd_hbm, wd)))
     ]
+    members = []
+    for i in range(3):
+        at = pl.ds(i * width, width)
+        members.append(pltpu.make_async_copy(wq_hbm.at[0, :, at], wq.at[:, at], w_sem.at[3 + i]))
     take_x = pltpu.make_async_copy(x_hbm, hb, o_sem.at[3])
     take_ct = pltpu.make_async_copy(ct_hbm, eb, o_sem.at[3])
 
@@ -92,7 +96,7 @@
     def _():
         take_ct.start()
 
-    for copy in weights:
+    for copy in members:
         copy.start()
 
     barrier = pltpu.get_barrier_semaphore()
@@ -140,7 +144,7 @@
         return y_hop(4, mask, mask2)
 
     def bit_of(level, t):
-        return jnp.where(t % 3 == 2, 1 - level, level) if level < 2 else level
+        return jnp.where(t % 3 == 1, 1 - level, level) if level < 2 else level
 
     def half_of(level, t):
         return me // (1 << bit_of(level, t)) % 2 if level >= 2 else jnp.where(bit_of(level, t) == 0, me % 2, me // 2 % 2)
@@ -224,15 +228,24 @@
     row_loop(first_norm)
 
     y_act(A, ab).start()
-    weights[0].wait()
-
     def cols_of(t):
         return pl.ds(pl.multiple_of(t * TILE, TILE), TILE)
 
     def project(t, at):
         pb[:, at] = mul(ab[...], wq[:, at]).astype(bf16)
 
-    tile_loop(q_tiles, project)
+    for i, copy in enumerate(members):
+        copy.wait()
+
+        if i == 1:
+            for rest_copy in weights:
+                rest_copy.start()
+
+        def project_member(t, _):
+            project(t, cols_of(i * o_tiles + t))
+
+        tile_loop(o_tiles, project_member)
+
 
     def pairs_of(first, count):
         return [(b, first + u, u) for u in range(count) for b in range(blocks)]
@@ -261,7 +274,7 @@
             store[tile_at(first, b, u)] = mul(chance, part(b, 2, h)).astype(bf16)
 
     attend(pairs_of(0, heads), mask, ra, O_AT)
-    weights[1].wait()
+    weights[0].wait()
 
     def attention_out(t, at):
         total = hb[:, at].astype(f32)
@@ -280,7 +293,7 @@
     row_loop(second_norm)
 
     y_act(C, cb).start()
-    weights[2].wait()
+    weights[1].wait()
 
     def feed_up(t, at, source, store, first):
         value, slope = gelu_pair(mul(source[...], wu[:, at]))
@@ -288,7 +301,7 @@
         gp[:, at] = slope
 
     tile_loop(u_tiles, partial(feed_up, source=cb, store=ra, first=G_AT))
-    weights[3].wait()
+    weights[2].wait()
 
     def feed_down(t, at):
         total = mm[:, at]
@@ -324,7 +337,7 @@
         transpose_into(lt, E, eb)
 
     def piece(v, j, t):
-        alt = t % 3 == 2
+        alt = t % 3 == 1
         return jnp.where(alt, j % 2, v), jnp.where(alt, j // 2 * 2 + v, j)
 
     def product(t, v):
@@ -482,7 +495,7 @@
         feed_half()
 
     tile_loop(u_half, half_down_back)
-    merge_range(0, 4)
+    merge_range(0, 2)
 
     def half_project(t, _):
         at = cols_of(t // o_half * o_tiles + rep * o_half + t % o_half)
@@ -495,7 +508,7 @@
     y_act(DM, dmb).wait_recv()
     transpose_into(ltr, DM, pin.at[DM])
     open_range(OUT * per_tile, QKV * per_tile)
-    merge_range(4, 6)
+    merge_range(2, 3)
 
     def half_out_back(t, _):
         attention_out_back(t, cols_of(rep * o_half + t), pin.at[DM])
@@ -522,15 +535,15 @@
         def _():
             open_tile(s + opened)
 
-        @pl.when(s + 6 < cuts)
-        def _():
-            merge(0, s + 6)
-
-        for level, lag in enumerate(lags[1:], 1):
+        for level, lag in reversed(list(enumerate(lags[1:], 1))):
 
             @pl.when((s >= lag) & (s < cuts + lag))
             def _():
                 merge(level, s - lag)
+
+        @pl.when(s + 3 < cuts)
+        def _():
+            merge(0, s + 3)
 
         for n in range(levels + 1):
 
@@ -547,16 +560,24 @@
     else:
         small_ref[...] = small[2 * levels + 2]
 
+    def take_cut(t):
+        return pltpu.make_async_copy(ag.at[:, t], grad_hbm.at[:, t], o_sem.at[4 + t])
+
+    def finish_cut(t, carry):
+        g_tile(t).wait_recv()
+        take_cut(t).start()
+        return carry
+
+    lax.fori_loop(0, cuts, finish_cut, 0)
+
     def drain(t, carry):
-        g_tile(t).wait_recv()
+        take_cut(t).wait()
         for level in range(levels):
             x_tile(level, t).wait_send()
         g_tile(t).wait_send()
         return carry
 
     lax.fori_loop(0, cuts, drain, 0)
-    grads_copy = pltpu.make_async_copy(ag, grad_hbm, o_sem.at[2])
-    grads_copy.start()
     y_mask().wait_send()
     for n in (A, DM, C):
         y_act(n, ab).wait_send()
@@ -576,7 +597,6 @@
 
     out_copy.wait()
     dh_copy.wait()
-    grads_copy.wait()
 
 
 def finish_kernel(
@@ -611,7 +631,7 @@
             piece = raw[r, first + c]
             cols = slice(at + c * CUT, at + (c + 1) * CUT)
             if turned and turn:
-                buffer[cols, :] = piece.astype(f32).T
+                buffer[cols, :] = piece.T.astype(f32)
             else:
                 buffer[:, cols] = piece.astype(f32)
         size = count * CUT
@@ -671,7 +691,7 @@
         vm((cuts, dp // 2, shard, CUT), bf16),
         *[vm((cuts, 2, dp >> (level + 1), shard, CUT), bf16) for level in range(1, levels)],
         *[vm((cuts, dp >> (level + 1), shard, CUT), bf16) for level in range(levels)],
-        dma((4,)), dma((4,)),
+        dma((6,)), dma((4 + cuts,)),
         dma((5,)), dma((5,)),
         dma((levels, cuts)), dma((levels, cuts)),
         dma((cuts,)), dma((cuts,)),

time: 145 us -> 143 us (0.986)
  Pallas kernels: 144 us -> 142 us
    pallas_call x1, Pallas kernels: 139 us -> 137 us  [per_device(): pl.pallas_call(step_kernel, out_shape=(sds((rows, width), bf16), sds((row...]
where the time goes in v3:
time: 143 us
  Pallas kernels  142 us (99%)
    pallas_call x1, Pallas kernels, per_device(): pl.pallas_call(step_kernel, out_shape=(sds((rows, width), bf16), sds((row...  137 us
    pallas_call x1, Pallas kernels, per_device(): pl.pallas_call(partial(finish_kernel, whole_lanes), out_shape=[sds((1, *s...  4.84 us

profile of v3, /device:TPU:0, one launch (start us, length us, event | category | flops | bytes accessed | tf_op | source)
XLA Modules:
  0.0 142.6 jit_solution(14315091913829561442)
XLA Ops:
  0.6 137.0 %layers_step.1 = (bf16[256,1024]{1,0:T(8,128)(2,1)}, bf16[256,1024]{1,0:T(8,128)(2,1)}, bf16[2,16,128,256]{3,2,1,0:T(8,128)(2,1)}, f32[8,128]{1,0:T(8,128)}) custom-call(bf16[256,1024]{1,0:T(8,128)(2,1)} %x_hbm.1, bf16[256,1024]{1,0:T(8,128)(2,1)} %ct_hbm.1, s32[16]{0:T(128)} %count_ref.1, bf16[1,1024,3072]{2,1,0:T(8,128)(2,1)} %wq_hbm.1, ...), custom_call_target="tpu_custom_call" | custom-call | tf_op jit(solution)/shard_map/layers_step/pallas_call | solution.py:704
  137.6 4.8 %finish.1 = (f32[1,128,3072]{2,1,0:T(8,128)}, f32[1,1024,128]{2,1,0:T(8,128)}, f32[1,128,2048]{2,1,0:T(8,128)}, f32[1,2048,128]{2,1,0:T(8,128)}, bf16[1,256,1024...) custom-call(bf16[2,16,128,256]{3,2,1,0:T(8,128)(2,1)} %get-tuple-element.20.grad_hb, ...), custom_call_target="tpu_custom_call" | custom-call | tf_op jit(solution)/shard_map/finish/pallas_call | solution.py:726

commit v4 on v3

--- a/solution.py
+++ b/solution.py
@@ -495,7 +495,7 @@
         feed_half()
 
     tile_loop(u_half, half_down_back)
-    merge_range(0, 2)
+    merge_range(0, 3)
 
     def half_project(t, _):
         at = cols_of(t // o_half * o_tiles + rep * o_half + t % o_half)
@@ -508,7 +508,7 @@
     y_act(DM, dmb).wait_recv()
     transpose_into(ltr, DM, pin.at[DM])
     open_range(OUT * per_tile, QKV * per_tile)
-    merge_range(2, 3)
+    merge_range(3, 4)
 
     def half_out_back(t, _):
         attention_out_back(t, cols_of(rep * o_half + t), pin.at[DM])
@@ -541,9 +541,9 @@
             def _():
                 merge(level, s - lag)
 
-        @pl.when(s + 3 < cuts)
+        @pl.when(s + 4 < cuts)
         def _():
-            merge(0, s + 3)
+            merge(0, s + 4)
 
         for n in range(levels + 1):
 

time: 143 us -> 143 us (level)
  no operation moved by 1% of the time
where the time goes in v4:
time: 143 us; the launch traced here: 142 us
  Pallas kernels  142 us (99%)
    pallas_call x1, Pallas kernels, per_device(): pl.pallas_call(step_kernel, out_shape=(sds((rows, width), bf16), sds((row...  137 us
    pallas_call x1, Pallas kernels, per_device(): pl.pallas_call(partial(finish_kernel, whole_lanes), out_shape=[sds((1, *s...  4.84 us

profile of v4, /device:TPU:0, one launch (start us, length us, event | category | flops | bytes accessed | tf_op | source)
XLA Modules:
  0.0 142.4 jit_solution(14240871659179460092)
XLA Ops:
  0.6 136.8 %layers_step.1 = (bf16[256,1024]{1,0:T(8,128)(2,1)}, bf16[256,1024]{1,0:T(8,128)(2,1)}, bf16[2,16,128,256]{3,2,1,0:T(8,128)(2,1)}, f32[8,128]{1,0:T(8,128)}) custom-call(bf16[256,1024]{1,0:T(8,128)(2,1)} %x_hbm.1, bf16[256,1024]{1,0:T(8,128)(2,1)} %ct_hbm.1, s32[16]{0:T(128)} %count_ref.1, bf16[1,1024,3072]{2,1,0:T(8,128)(2,1)} %wq_hbm.1, ...), custom_call_target="tpu_custom_call" | custom-call | tf_op jit(solution)/shard_map/layers_step/pallas_call | solution.py:704
  137.4 4.8 %finish.1 = (f32[1,128,3072]{2,1,0:T(8,128)}, f32[1,1024,128]{2,1,0:T(8,128)}, f32[1,128,2048]{2,1,0:T(8,128)}, f32[1,2048,128]{2,1,0:T(8,128)}, bf16[1,256,1024...) custom-call(bf16[2,16,128,256]{3,2,1,0:T(8,128)(2,1)} %get-tuple-element.20.grad_hb, ...), custom_call_target="tpu_custom_call" | custom-call | tf_op jit(solution)/shard_map/finish/pallas_call | solution.py:726
